TPU v7x, 32 devices: a whole 2x2x4 slice. The times are simulated.
32 devices in a mesh: sec: 4 (over y, x), seq: 8 (over z, core).
Axes of the slice: x: 2, y: 2, z: 4, core: 2. Of those that a mesh axis runs over, the one named last changes fastest.
Arguments:
- long_queries: bfloat16 [16, 4096], P('sec'), may hold values from -15 to 15
- long_keys: bfloat16 [512, 16, 2048], P(('sec', 'seq')), may hold values from -6 to 6
- long_values: bfloat16 [512, 16, 2048], P(('sec', 'seq')), may hold values from -6 to 6
- page_table: int32 [16, 32], replicated, may hold values from 0 to 511, as said below
- long_lengths: int32 [16], replicated, may hold values from 1 to 512, 5120 in all
- short_queries: bfloat16 [32, 256], P(('sec', 'seq')), may hold values from -15 to 15
- short_keys: bfloat16 [32, 2048, 128], P(('sec', 'seq')), may hold values from -6 to 6
- short_values: bfloat16 [32, 2048, 128], P(('sec', 'seq')), may hold values from -6 to 6
- short_lengths: int32 [2], replicated, may hold values from 1 to 2048, 2560 in all
- out_weight: bfloat16 [4096, 4608], P('seq', 'sec'), may hold values from -0.09375 to 0.09375
- long_resid: bfloat16 [16, 4608], P(None, 'sec'), may hold values from -1.5 to 1.5
Outputs:
- long_out: bfloat16 [16, 4608], P(None, 'sec')
- short_out: bfloat16 [32, 256], P(('sec', 'seq'))
Inputs may be any that keep to these rules, and one draw needn't show every extreme that they name: `page_table`: row r lists the 32 pool pages of long request r in order of position; every page of the pool of 512 appears exactly once; page g is held by device g // 16 along sec+seq. `long_lengths`: counts the newest token; later slots are unused. `short_lengths`: counts the newest token; later slots are unused.
All inputs are finite; a program needn't handle non-finite values.
Results may differ from a plain program's by a relative error of at most 0.0055.
Values may be sent and summed in bfloat16 or wider, within the bound.
A program may use at most 64 MiB of HBM per device.

v0:
```python
import jax
import jax.numpy as jnp
from jax import lax
from jax.sharding import PartitionSpec as P

KVH = 16
HD = 128
G = 2


soft_cap = 50.0
score_scale = 144.0 ** (-0.5)


def capped_weights(raw_scores, live_mask):
    capped = soft_cap * jnp.tanh(raw_scores * (score_scale / soft_cap))
    return jnp.where(live_mask, jnp.exp(capped), 0.0)


def per_device(
    long_queries,
    long_keys,
    long_values,
    page_table,
    long_lengths,
    short_queries,
    short_keys,
    short_values,
    short_lengths,
    out_weight,
    long_resid,
):
    queries = lax.all_gather(long_queries, "sec", axis=0, tiled=True)
    requests = queries.shape[0]
    page_count, page_len, kv_width = long_keys.shape
    tokens = page_count * page_len
    head_count = KVH * G
    first_page = lax.axis_index(("sec", "seq")) * page_count
    page_ids = first_page + jnp.arange(page_count, dtype=jnp.int32)
    matched = page_table[:, :, None] == page_ids[None, None, :]
    page_held = jnp.any(matched, axis=1)
    slot_index = jnp.arange(page_table.shape[1], dtype=jnp.int32)
    slot_of = jnp.sum(jnp.where(matched, slot_index[None, :, None], 0), axis=1)
    position = slot_of[:, :, None] * page_len + jnp.arange(page_len, dtype=jnp.int32)[None, None, :]
    live_mask = page_held[:, :, None] & (position < long_lengths[:, None, None])
    live_mask = live_mask.reshape(requests, tokens)
    grouped = (
        queries.reshape(requests, KVH, G, HD).transpose(1, 0, 2, 3).reshape(KVH, requests * G, HD)
    )
    key_rows = long_keys.reshape(tokens, KVH, HD)
    value_rows = long_values.reshape(tokens, KVH, HD)
    raw_scores = jnp.einsum("hqd,thd->hqt", grouped, key_rows, preferred_element_type=jnp.float32)
    token_mask = jnp.broadcast_to(live_mask[None, :, None, :], (KVH, requests, G, tokens)).reshape(
        KVH, requests * G, tokens
    )
    weights = capped_weights(raw_scores, token_mask)
    totals = jnp.sum(weights, axis=2)
    part_sums = jnp.einsum(
        "hqt,thd->hqd", weights.astype(jnp.bfloat16), value_rows, preferred_element_type=jnp.float32
    )
    part_sums = (
        part_sums.reshape(KVH, requests, G, HD)
        .transpose(1, 0, 2, 3)
        .reshape(requests, head_count * HD)
    )
    totals = totals.reshape(KVH, requests, G).transpose(1, 0, 2).reshape(requests, head_count)
    share_width = out_weight.shape[0]
    share_start = lax.axis_index("seq") * share_width
    part_sums, totals = lax.psum((part_sums, totals), ("sec", "seq"))
    attention = (
        (part_sums.reshape(requests, head_count, HD) / totals[:, :, None])
        .astype(jnp.bfloat16)
        .reshape(requests, head_count * HD)
    )
    feature_rows = lax.dynamic_slice_in_dim(attention, share_start, share_width, 1)
    partial_proj = jnp.dot(feature_rows, out_weight, preferred_element_type=jnp.float32)
    projected = lax.psum(partial_proj, "seq")
    long_out = (long_resid.astype(jnp.float32) + projected).astype(jnp.bfloat16)
    pair_count = short_queries.shape[0]
    length = short_keys.shape[1]
    pair_ids = lax.axis_index(("sec", "seq")) * pair_count + jnp.arange(pair_count, dtype=jnp.int32)
    request_of = pair_ids // KVH
    chosen = request_of[:, None] == jnp.arange(short_lengths.shape[0], dtype=jnp.int32)[None, :]
    pair_limit = jnp.sum(jnp.where(chosen, short_lengths[None, :], 0), axis=1)
    short_live = jnp.arange(length, dtype=jnp.int32)[None, :] < pair_limit[:, None]
    pair_queries = short_queries.reshape(pair_count, G, HD)
    short_scores = jnp.einsum(
        "pgd,ptd->pgt", pair_queries, short_keys, preferred_element_type=jnp.float32
    )
    short_weights = capped_weights(short_scores, short_live[:, None, :])
    short_totals = jnp.sum(short_weights, axis=2)
    short_sums = jnp.einsum(
        "pgt,ptd->pgd",
        short_weights.astype(jnp.bfloat16),
        short_values,
        preferred_element_type=jnp.float32,
    )
    short_out = (
        (short_sums / short_totals[:, :, None]).astype(jnp.bfloat16).reshape(pair_count, G * HD)
    )
    return (long_out, short_out)


def solution(mesh):
    in_specs = (
        P("sec", None),
        P(("sec", "seq"), None, None),
        P(("sec", "seq"), None, None),
        P(),
        P(),
        P(("sec", "seq"), None),
        P(("sec", "seq"), None, None),
        P(("sec", "seq"), None, None),
        P(),
        P("seq", "sec"),
        P(None, "sec"),
    )
    out_specs = (P(None, "sec"), P(("sec", "seq"), None))
    return jax.shard_map(
        per_device, mesh=mesh, in_specs=in_specs, out_specs=out_specs, check_vma=False
    )
```

profile of v0, /device:TPU:0, one launch (start us, length us, event | category | flops | bytes accessed | tf_op | source)
XLA Modules:
  0.0 212.0 jit_solution(14925022806387552283)
XLA Ops:
  7.2 1.2 fusion.16
  8.4 1.1 compare_reduce_fusion
  9.6 0.1 add.56
  9.7 0.1 add.57
  9.8 0.1 and.21
  9.9 0.1 and.22
  10.0 0.1 add.59
  10.1 0.7 fusion.20
  10.9 1.5 copy.36
  12.5 9.9 %all-gather = bf16[4,4,4096]{2,1,0:T(4,128)(2,1)S(1)} all-gather(bf16[1,4,4096]{2,1,0:T(4,128)(2,1)S(1)} %bitcast.58), channel_id=1, replica_groups=mesh['sec'=4,'seq'=8] {'sec'}, dimensions={0}, use_global_device_ids=true | all-gather | bytes 163840 | tf_op jit(solution)/shard_map/all_gather | solution.py:33
  22.4 0.2 reshape.129
  22.6 0.1 copy.29
  22.7 0.2 copy.37
  22.9 0.6 fusion.25
  23.5 0.3 fusion.10
  23.9 0.1 copy.50
  24.0 0.9 reshape.134
  25.0 0.6 fusion.22
  25.7 0.7 iota_compare_fusion
  26.3 0.1 copy.33
  26.4 0.1 copy.34
  26.5 39.5 %psum.22 = f32[16,32]{0,1:T(8,128)S(1)} all-reduce(f32[16,32]{0,1:T(8,128)S(1)} %bitcast.57), channel_id=1, replica_groups=mesh['sec'=4,'seq'=8] {'sec','seq'}, use_global_device_ids=true, to_apply=%region_4.5 | all-reduce | flops 512 | bytes 4096 | tf_op jit(solution)/shard_map/psum | solution.py:69
  66.0 0.1 copy.35
  66.0 0.1 div.30
  66.2 0.2 copy.49
  66.4 0.4 fusion.26
  66.8 85.2 %all-reduce.3.cloned.1.call-done = f32[16,4096]{1,0:T(8,128)} async-done(((f32[16,4096]{1,0:T(8,128)}), f32[16,4096]{1,0:T(8,128)}) %all-reduce.3.cloned.1.call-update) | async-done | bytes 262160 | tf_op jit(solution)/shard_map/psum | solution.py:69
  152.0 1.6 fusion.18
  153.7 0.2 fusion.9
  153.9 0.6 copy.51
  154.5 49.1 %all-reduce.5.cloned.1.call-done = f32[16,1152]{1,0:T(8,128)} async-done(((f32[16,1152]{1,0:T(8,128)}), f32[16,1152]{1,0:T(8,128)}) %all-reduce.5.cloned.1.call-update) | async-done | bytes 73744 | tf_op jit(solution)/shard_map/psum | solution.py:77
  203.6 1.5 add_convert_fusion
  (26 shorter events, 0.2 us)
Async XLA Ops:
  7.2 144.8 %copy-start = (bf16[512,1152]{1,0:T(8,128)(2,1)S(1)}, bf16[512,1152]{1,0:T(8,128)(2,1)}, u32[]{:S(2)}) copy-start(bf16[512,1152]{1,0:T(8,128)(2,1)} %param.20) | copy-start | bytes 3538948
  7.2 144.8 %all-reduce.3.cloned.1.call-start = ((), (), s32[]{:S(2)}) async-start(), calls=%async_computation | async-start | bytes 524288 | tf_op jit(solution)/shard_map/psum | solution.py:69
  9.7 2.8 %copy-start.4 = (bf16[4,4096]{1,0:T(4,128)(2,1)S(1)}, bf16[4,4096]{1,0:T(4,128)(2,1)}, u32[]{:S(2)}) copy-start(bf16[4,4096]{1,0:T(4,128)(2,1)} %param.11) | copy-start | bytes 98308
  10.9 11.8 %copy-start.1 = (bf16[16,16,2048]{2,1,0:T(8,128)(2,1)S(1)}, bf16[16,16,2048]{2,1,0:T(8,128)(2,1)}, u32[]{:S(2)}) copy-start(bf16[16,16,2048]{2,1,0:T(8,128)(2,1)} %param.13) | copy-start | bytes 3145732
  23.5 1.5 copy-start.7
  23.8 42.5 %copy-start.5 = (bf16[1,256]{1,0:T(2,128)(2,1)S(1)}, bf16[1,256]{1,0:T(2,128)(2,1)}, u32[]{:S(2)}) copy-start(bf16[1,256]{1,0:T(2,128)(2,1)} %param.16) | copy-start | bytes 1540
  23.9 42.5 %copy-start.2 = (bf16[1,2048,128]{2,1,0:T(8,128)(2,1)S(1)}, bf16[1,2048,128]{2,1,0:T(8,128)(2,1)}, u32[]{:S(2)}) copy-start(bf16[1,2048,128]{2,1,0:T(8,128)(2,1)} %param.17) | copy-start | bytes 1572868
  24.9 178.7 %all-reduce.5.cloned.1.call-start = ((), (), s32[]{:S(2)}) async-start(), calls=%async_computation.1 | async-start | bytes 147456 | tf_op jit(solution)/shard_map/psum | solution.py:77
  66.2 87.5 %copy-start.6 = (bf16[1,2048,128]{2,1,0:T(8,128)(2,1)S(1)}, bf16[1,2048,128]{2,1,0:T(8,128)(2,1)}, u32[]{:S(2)}) copy-start(bf16[1,2048,128]{2,1,0:T(8,128)(2,1)} %param.18) | copy-start | bytes 1572868
  66.4 137.2 %copy-start.3 = (bf16[16,1152]{1,0:T(8,128)(2,1)S(1)}, bf16[16,1152]{1,0:T(8,128)(2,1)}, u32[]{:S(2)}) copy-start(bf16[16,1152]{1,0:T(8,128)(2,1)} %param.21) | copy-start | bytes 110596
Sparse Core Ops, SparseCore 0:
  25.1 126.8 all-reduce.2
  154.3 49.2 all-reduce.4
where the time goes:
time: 213 us; the launch traced here: 212 us
  waiting for transfers between devices  134 us (63%)
  blocking collectives  49.4 us (23%)
  between operations  14.3 us (7%)
  other arithmetic  5.86 us (3%)
  local copies, waits for them, and re-layouts  4.75 us (2%)
  matrix products  3.13 us (1%)
    psum x1, waiting for transfers between devices, per_device(): part_sums, totals = lax.psum((part_sums, totals), ('sec', 'seq'))  85.2 us
    psum x1, waiting for transfers between devices, per_device(): projected = lax.psum(partial_proj, 'seq')  49.1 us
    psum x1, blocking collectives, per_device(): part_sums, totals = lax.psum((part_sums, totals), ('sec', 'seq'))  39.5 us
    all_gather x1, blocking collectives, per_device(): queries = lax.all_gather(long_queries, 'sec', axis=0, tiled=True)  9.94 us
  transfers between devices with their start and end apart: 2, of which 2 were waited for; matrix products, arithmetic and copies ran while one was open for 1% of the time, Pallas kernels for 0%

commit v1 on v0

--- a/solution.py
+++ b/solution.py
@@ -1,6 +1,9 @@
+import functools
 import jax
 import jax.numpy as jnp
 from jax import lax
+from jax.experimental import pallas as pl
+from jax.experimental.pallas import tpu as pltpu
 from jax.sharding import PartitionSpec as P
 
 KVH = 16
@@ -101,6 +104,433 @@
     return (long_out, short_out)
 
 
+MESH = pl.DeviceIdType.MESH
+CONTRACT_LAST = (((1,), (1,)), ((), ()))
+
+
+def decode_kernel(
+    n_sec,
+    n_seq,
+    page_len,
+    q_ref,
+    k_hbm,
+    v_hbm,
+    table_ref,
+    lens_ref,
+    sq_ref,
+    sk_hbm,
+    sv_hbm,
+    slens_ref,
+    w_hbm,
+    resid_ref,
+    long_ref,
+    short_ref,
+    k_ref,
+    v_ref,
+    sk_ref,
+    sv_ref,
+    w_ref,
+    q_slabs,
+    q_rows,
+    mask_ref,
+    part_send,
+    part_recv,
+    part_own,
+    sec_buf,
+    pair_send,
+    pair_recv,
+    z_buf,
+    fin_buf,
+    load_sem,
+    q_send_sem,
+    q_recv_sem,
+    a_send_sem,
+    a_recv_sem,
+    b_send_sem,
+    b_recv_sem,
+    c_send_sem,
+    c_recv_sem,
+    z_send_sem,
+    z_recv_sem,
+    f_send_sem,
+    f_recv_sem,
+):
+    sec = lax.axis_index("sec")
+    seq = lax.axis_index("seq")
+    core = lax.rem(seq, 2)
+    deep = seq // 2
+    n_deep = n_seq // 2
+    mate = seq + 1 - 2 * core
+    sec_peers = [lax.rem(sec + i, n_sec) for i in range(1, n_sec)]
+    seq_peers = [lax.rem(seq + i, n_seq) for i in range(1, n_seq)]
+
+    barrier = pltpu.get_barrier_semaphore()
+    for peer in sec_peers:
+        pl.semaphore_signal(barrier, inc=1, device_id={"sec": peer}, device_id_type=MESH)
+    for peer in seq_peers:
+        pl.semaphore_signal(barrier, inc=1, device_id={"seq": peer}, device_id_type=MESH)
+
+    loads = []
+    for i, (src, dst) in enumerate(
+        (
+            (q_ref, q_slabs.at[sec]),
+            (sk_hbm, sk_ref),
+            (sv_hbm, sv_ref),
+            (k_hbm, k_ref),
+            (v_hbm, v_ref),
+            (w_hbm, w_ref),
+        )
+    ):
+        copy = pltpu.make_async_copy(src, dst, load_sem.at[i])
+        copy.start()
+        loads.append(copy)
+
+    slab_rows = q_ref.shape[0]
+    requests, slots = table_ref.shape
+    tokens = k_ref.shape[0]
+    page_count = tokens // page_len
+    first_page = (sec * n_seq + seq) * page_count
+    token = lax.broadcasted_iota(jnp.int32, (requests, tokens), 1)
+    row = lax.broadcasted_iota(jnp.int32, (requests, tokens), 0)
+    page_of = first_page + token // page_len
+    slot_of = jnp.full((requests, tokens), 1 << 20, jnp.int32)
+    table = table_ref[...]
+    for s in range(slots):
+        slot_of = jnp.where(table[:, s : s + 1] == page_of, s, slot_of)
+    limits = jnp.zeros((requests, tokens), jnp.int32)
+    for r in range(requests):
+        limits = jnp.where(row == r, lens_ref[r], limits)
+    position = slot_of * page_len + lax.rem(token, page_len)
+    live = jnp.where(position < limits, 1.0, 0.0).astype(jnp.float32)
+    for g in range(G):
+        mask_ref[g * requests : (g + 1) * requests, :] = live
+
+    pl.semaphore_wait(barrier, n_sec + n_seq - 2)
+    loads[0].wait()
+    q_copies = []
+    for i, peer in enumerate(sec_peers):
+        copy = pltpu.make_async_remote_copy(
+            src_ref=q_ref,
+            dst_ref=q_slabs.at[sec],
+            send_sem=q_send_sem.at[i],
+            recv_sem=q_recv_sem.at[sec],
+            device_id={"sec": peer},
+            device_id_type=MESH,
+        )
+        copy.start()
+        q_copies.append(copy)
+
+    factor = score_scale / soft_cap
+    loads[1].wait()
+    loads[2].wait()
+    pair_count = sq_ref.shape[0]
+    length = sk_ref.shape[0] // pair_count
+    short_at = lax.broadcasted_iota(jnp.int32, (8, length), 1)
+    which = lax.broadcasted_iota(jnp.int32, (8, HD), 0)
+    for p in range(pair_count):
+        pair_id = (sec * n_seq + seq) * pair_count + p
+        limit = slens_ref[pair_id // KVH]
+        q_pair = sq_ref[p : p + 1, :].astype(jnp.float32)
+        stacked = jnp.zeros((8, HD), jnp.float32)
+        for g in range(G):
+            stacked = jnp.where(which == g, q_pair[:, g * HD : (g + 1) * HD], stacked)
+        raw = lax.dot_general(
+            stacked.astype(jnp.bfloat16),
+            sk_ref[p * length : (p + 1) * length, :],
+            CONTRACT_LAST,
+            preferred_element_type=jnp.float32,
+        )
+        weights = jnp.where(short_at < limit, jnp.exp(soft_cap * jnp.tanh(raw * factor)), 0.0)
+        totals = jnp.sum(weights, axis=1, keepdims=True)
+        sums = jnp.dot(
+            weights.astype(jnp.bfloat16),
+            sv_ref[p * length : (p + 1) * length, :],
+            preferred_element_type=jnp.float32,
+        )
+        result = (sums / totals).astype(short_ref.dtype)
+        for g in range(G):
+            short_ref[p : p + 1, g * HD : (g + 1) * HD] = result[g : g + 1, :]
+
+    loads[3].wait()
+    loads[4].wait()
+    for i, peer in enumerate(sec_peers):
+        pltpu.make_async_remote_copy(
+            src_ref=q_ref,
+            dst_ref=q_slabs.at[peer],
+            send_sem=q_send_sem.at[i],
+            recv_sem=q_recv_sem.at[peer],
+            device_id={"sec": peer},
+            device_id_type=MESH,
+        ).wait_recv()
+    for s in range(n_sec):
+        q_rows[s * slab_rows : (s + 1) * slab_rows, :] = q_slabs[s].astype(jnp.float32)
+
+    share = w_ref.shape[0]
+    heads = share // (G * HD)
+    blocks = share // HD
+    lane = lax.broadcasted_iota(jnp.int32, (requests, HD), 1)
+    a_copies = []
+    half = n_seq // 2
+    order = [half]
+    for i in range(1, half):
+        order += [half + i, half - i]
+    order.append(0)
+    mask = mask_ref[...]
+    for step, offset in enumerate(order):
+        dest = lax.rem(seq + offset, n_seq) if offset else seq
+        total_block = jnp.zeros((requests, HD), jnp.float32)
+        for a in range(heads):
+            at = pl.multiple_of(dest * share + a * G * HD, G * HD)
+            kv_at = pl.multiple_of((dest * heads + a) * HD, HD)
+            q_now = jnp.concatenate(
+                [q_rows[:, pl.ds(pl.multiple_of(at + g * HD, HD), HD)] for g in range(G)], axis=0
+            ).astype(jnp.bfloat16)
+            raw = lax.dot_general(
+                q_now,
+                k_ref[:, pl.ds(kv_at, HD)],
+                CONTRACT_LAST,
+                preferred_element_type=jnp.float32,
+            )
+            weights = jnp.exp(soft_cap * jnp.tanh(raw * factor)) * mask
+            totals = jnp.sum(weights, axis=1, keepdims=True)
+            sums = jnp.dot(
+                weights.astype(jnp.bfloat16),
+                v_ref[:, pl.ds(kv_at, HD)],
+                preferred_element_type=jnp.float32,
+            )
+            for g in range(G):
+                b = a * G + g
+                piece = sums[g * requests : (g + 1) * requests, :]
+                total = totals[g * requests : (g + 1) * requests, :]
+                total_block = jnp.where(lax.rem(lane, blocks) == b, total, total_block)
+                if offset:
+                    part_send[step, :, b * HD : (b + 1) * HD] = piece.astype(jnp.bfloat16)
+                else:
+                    part_own[:, b * HD : (b + 1) * HD] = piece
+        if offset:
+            high = total_block.astype(jnp.bfloat16)
+            low = (total_block - high.astype(jnp.float32)).astype(jnp.bfloat16)
+            part_send[step, :, share : share + HD] = jnp.where(
+                lane < blocks, high.astype(jnp.float32), low.astype(jnp.float32)
+            ).astype(jnp.bfloat16)
+            copy = pltpu.make_async_remote_copy(
+                src_ref=part_send.at[step],
+                dst_ref=part_recv.at[n_seq - offset],
+                send_sem=a_send_sem.at[step],
+                recv_sem=a_recv_sem.at[n_seq - offset],
+                device_id={"seq": dest},
+                device_id_type=MESH,
+            )
+            copy.start()
+            a_copies.append(copy)
+        else:
+            part_own[:, share : share + HD] = jnp.where(lane < blocks, total_block, 0.0)
+
+    gathered = part_own[...]
+    for copy, offset in zip(a_copies, order):
+        pltpu.make_async_remote_copy(
+            src_ref=part_send.at[0],
+            dst_ref=part_recv.at[offset],
+            send_sem=a_send_sem.at[0],
+            recv_sem=a_recv_sem.at[offset],
+            device_id={"seq": seq_peers[0]},
+            device_id_type=MESH,
+        ).wait_recv()
+        gathered = gathered + part_recv[offset].astype(jnp.float32)
+
+    totals_part = gathered[:, share : share + HD]
+    totals_part = totals_part + pltpu.roll(totals_part, HD - blocks, 1)
+    repeated = totals_part
+    for i in range(1, 2):
+        repeated = jnp.where(lane < blocks, repeated, pltpu.roll(totals_part, blocks, 1))
+    high = repeated.astype(jnp.bfloat16).astype(jnp.float32)
+    tail_block = jnp.where(lane < blocks, high, repeated - high)
+    sec_buf[0, :, 0:share] = gathered[:, 0:share].astype(jnp.bfloat16)
+    sec_buf[0, :, share : share + HD] = tail_block.astype(jnp.bfloat16)
+    b_copies = []
+    for i, peer in enumerate(sec_peers):
+        copy = pltpu.make_async_remote_copy(
+            src_ref=sec_buf.at[0],
+            dst_ref=sec_buf.at[n_sec - 1 - i],
+            send_sem=b_send_sem.at[i],
+            recv_sem=b_recv_sem.at[n_sec - 1 - i],
+            device_id={"sec": peer},
+            device_id_type=MESH,
+        )
+        copy.start()
+        b_copies.append(copy)
+    sums_now = gathered[:, 0:share]
+    totals_now = jnp.where(lane < blocks, totals_part, 0.0)
+    loads[5].wait()
+    for i in range(1, n_sec):
+        pltpu.make_async_remote_copy(
+            src_ref=sec_buf.at[0],
+            dst_ref=sec_buf.at[i],
+            send_sem=b_send_sem.at[0],
+            recv_sem=b_recv_sem.at[i],
+            device_id={"sec": sec_peers[0]},
+            device_id_type=MESH,
+        ).wait_recv()
+        arrived = sec_buf[i].astype(jnp.float32)
+        sums_now = sums_now + arrived[:, 0:share]
+        totals_now = totals_now + arrived[:, share : share + HD]
+    totals_now = totals_now + pltpu.roll(totals_now, HD - blocks, 1)
+    attention = jnp.concatenate(
+        [sums_now[:, b * HD : (b + 1) * HD] / totals_now[:, b : b + 1] for b in range(blocks)],
+        axis=1,
+    ).astype(jnp.bfloat16)
+    partial = jnp.dot(attention, w_ref[...], preferred_element_type=jnp.float32)
+
+    rows = requests // 2
+    upper, lower = partial[:rows, :], partial[rows:, :]
+    first = core == 0
+    pair_send[...] = jnp.where(first, lower, upper).astype(jnp.bfloat16)
+    c_copy = pltpu.make_async_remote_copy(
+        src_ref=pair_send,
+        dst_ref=pair_recv,
+        send_sem=c_send_sem,
+        recv_sem=c_recv_sem,
+        device_id={"seq": mate},
+        device_id_type=MESH,
+    )
+    c_copy.start()
+    mine = jnp.where(first, upper, lower)
+    resid = resid_ref[...].astype(jnp.float32)
+    resid = jnp.where(first, resid[:rows, :], resid[rows:, :])
+    c_copy.wait_recv()
+    z_buf[deep] = (mine + pair_recv[...].astype(jnp.float32)).astype(jnp.bfloat16)
+    z_copies = []
+    for i in range(1, n_deep):
+        peer = lax.rem(deep + i, n_deep)
+        copy = pltpu.make_async_remote_copy(
+            src_ref=z_buf.at[deep],
+            dst_ref=z_buf.at[deep],
+            send_sem=z_send_sem.at[i - 1],
+            recv_sem=z_recv_sem.at[deep],
+            device_id={"seq": peer * 2 + core},
+            device_id_type=MESH,
+        )
+        copy.start()
+        z_copies.append(copy)
+    for i in range(1, n_deep):
+        peer = lax.rem(deep + i, n_deep)
+        pltpu.make_async_remote_copy(
+            src_ref=z_buf.at[peer],
+            dst_ref=z_buf.at[peer],
+            send_sem=z_send_sem.at[i - 1],
+            recv_sem=z_recv_sem.at[peer],
+            device_id={"seq": peer * 2 + core},
+            device_id_type=MESH,
+        ).wait_recv()
+    for i in range(n_deep):
+        resid = resid + z_buf[i].astype(jnp.float32)
+    fin_buf[core] = resid.astype(jnp.bfloat16)
+    f_copy = pltpu.make_async_remote_copy(
+        src_ref=fin_buf.at[core],
+        dst_ref=fin_buf.at[core],
+        send_sem=f_send_sem,
+        recv_sem=f_recv_sem,
+        device_id={"seq": mate},
+        device_id_type=MESH,
+    )
+    f_copy.start()
+    for copy in q_copies + a_copies + b_copies + [c_copy] + z_copies:
+        copy.wait_send()
+    f_copy.wait()
+    for i in range(2):
+        long_ref[i * rows : (i + 1) * rows, :] = fin_buf[i]
+
+
+def per_device_fused(n_sec, n_seq, *args):
+    (
+        long_queries,
+        long_keys,
+        long_values,
+        page_table,
+        long_lengths,
+        short_queries,
+        short_keys,
+        short_values,
+        short_lengths,
+        out_weight,
+        long_resid,
+    ) = args
+    page_count, page_len, kv_width = long_keys.shape
+    tokens = page_count * page_len
+    pair_count, length, _ = short_keys.shape
+    slab, q_width = long_queries.shape
+    requests = slab * n_sec
+    share, columns = out_weight.shape
+    rows = requests // 2
+    packed = share + HD
+    bf16, f32 = jnp.bfloat16, jnp.float32
+    vmem = pl.BlockSpec(memory_space=pltpu.VMEM)
+    smem = pl.BlockSpec(memory_space=pltpu.SMEM)
+    hbm = pl.BlockSpec(memory_space=pltpu.HBM)
+    dma = pltpu.SemaphoreType.DMA
+    return pl.pallas_call(
+        functools.partial(decode_kernel, n_sec, n_seq, page_len),
+        out_shape=(
+            jax.ShapeDtypeStruct(long_resid.shape, bf16),
+            jax.ShapeDtypeStruct(short_queries.shape, bf16),
+        ),
+        in_specs=[vmem, hbm, hbm, vmem, smem, vmem, hbm, hbm, smem, hbm, vmem],
+        out_specs=(vmem, vmem),
+        scratch_shapes=[
+            pltpu.VMEM((tokens, kv_width), bf16),
+            pltpu.VMEM((tokens, kv_width), bf16),
+            pltpu.VMEM((pair_count * length, HD), bf16),
+            pltpu.VMEM((pair_count * length, HD), bf16),
+            pltpu.VMEM((share, columns), bf16),
+            pltpu.VMEM((n_sec, slab, q_width), bf16),
+            pltpu.VMEM((requests, q_width), f32),
+            pltpu.VMEM((G * requests, tokens), f32),
+            pltpu.VMEM((n_seq, requests, packed), bf16),
+            pltpu.VMEM((n_seq, requests, packed), bf16),
+            pltpu.VMEM((requests, packed), f32),
+            pltpu.VMEM((n_sec, requests, packed), bf16),
+            pltpu.VMEM((rows, columns), bf16),
+            pltpu.VMEM((rows, columns), bf16),
+            pltpu.VMEM((n_seq // 2, rows, columns), bf16),
+            pltpu.VMEM((2, rows, columns), bf16),
+            dma((6,)),
+            dma((n_sec,)),
+            dma((n_sec,)),
+            dma((n_seq,)),
+            dma((n_seq,)),
+            dma((n_sec,)),
+            dma((n_sec,)),
+            dma,
+            dma,
+            dma((n_seq // 2,)),
+            dma((n_seq // 2,)),
+            dma,
+            dma,
+        ],
+        compiler_params=pltpu.CompilerParams(collective_id=0, has_side_effects=True),
+    )(
+        long_queries,
+        long_keys.reshape(tokens, kv_width),
+        long_values.reshape(tokens, kv_width),
+        page_table,
+        long_lengths,
+        short_queries,
+        short_keys.reshape(pair_count * length, HD),
+        short_values.reshape(pair_count * length, HD),
+        short_lengths,
+        out_weight,
+        long_resid,
+    )
+
+
+def pick_body(n_sec, n_seq, *args):
+    share = args[9].shape[0]
+    requests = args[0].shape[0] * n_sec
+    if share % (G * HD) == 0 and n_seq % 2 == 0 and requests % 16 == 0:
+        return per_device_fused(n_sec, n_seq, *args)
+    return per_device(*args)
+
+
 def solution(mesh):
     in_specs = (
         P("sec", None),
@@ -116,6 +546,7 @@
         P(None, "sec"),
     )
     out_specs = (P(None, "sec"), P(("sec", "seq"), None))
+    body = functools.partial(pick_body, mesh.shape["sec"], mesh.shape["seq"])
     return jax.shard_map(
-        per_device, mesh=mesh, in_specs=in_specs, out_specs=out_specs, check_vma=False
-    )
+        body, mesh=mesh, in_specs=in_specs, out_specs=out_specs, check_vma=False
+    )

time: 213 us -> 29.9 us (0.14)
  waiting for transfers between devices: 134 us -> 0 us
  blocking collectives: 49.4 us -> 0 us
  Pallas kernels: 0 us -> 26.4 us
  between operations: 14.3 us -> 0.64 us
  other arithmetic: 5.86 us -> 0 us
  matrix products: 3.13 us -> 0 us
  local copies, waits for them, and re-layouts: 4.75 us -> 2.58 us
    psum x2 -> x0, waiting for transfers between devices: 134 us -> none  [the longest x1 85.2 us: per_device(): part_sums, totals = lax.psum((part_sums, totals), ('sec', 'seq'))]
    psum x1 -> x0, blocking collectives: 39.5 us -> none  [per_device(): part_sums, totals = lax.psum((part_sums, totals), ('sec', 'seq'))]
    pallas_call x0 -> x1, Pallas kernels: none -> 26.4 us  [per_device_fused(): pl.pallas_call(functools.partial(decode_kernel, n_sec, n_seq, page_len),...]
    all_gather x1 -> x0, blocking collectives: 9.94 us -> none  [per_device(): queries = lax.all_gather(long_queries, 'sec', axis=0, tiled=True)]
    dot_general x5 -> x0, matrix products: 3.13 us -> none  [the longest x1 1.65 us: per_device(): jnp.dot(feature_rows, out_weight, preferred_element_type=jnp.float32)]
  transfers between devices with their start and end apart: 2 -> 0, of which waited for: 2 -> 0; matrix products, arithmetic and copies ran while one was open for 1% -> 0% of each run, Pallas kernels for 0% -> 0%
where the time goes in v1:
time: 29.9 us; the launch traced here: 29.6 us
  Pallas kernels  26.4 us (88%)
  local copies, waits for them, and re-layouts  2.58 us (9%)
  between operations  0.64 us (2%)
    pallas_call x1, Pallas kernels, per_device_fused(): pl.pallas_call(functools.partial(decode_kernel, n_sec, n_seq, page_len),...  26.4 us
    unnamed x2, local copies, waits for them, and re-layouts  2.58 us

profile of v1, /device:TPU:0, one launch (start us, length us, event | category | flops | bytes accessed | tf_op | source)
XLA Modules:
  0.0 29.6 jit_solution(7811508575163159666)
XLA Ops:
  0.6 26.4 %shard_map.122 = (bf16[16,1152]{1,0:T(8,128)(2,1)}, bf16[1,256]{1,0:T(2,128)(2,1)}) custom-call(bf16[4,4096]{1,0:T(4,128)(2,1)} %q_ref.1, bf16[256,2048]{1,0:T(8,128)(2,1)} %bitcast.4, bf16[256,2048]{1,0:T(8,128)(2,1)} %bitcast.5, s32[16,32]{1,0:T(8,128)} %table_ref.1, s32[16]{0:T(128)} %lens_ref.1, bf16[1,256]{1,0:T(2,128)(2,1)} %sq_ref.1, ...), custom_call_target="tpu_custom_call" | custom-call | tf_op jit(solution)/shard_map/pallas_call | solution.py:471
  27.0 1.4 %copy.15 = bf16[16,1152]{1,0:T(8,128)(2,1)} copy(bf16[16,1152]{1,0:T(8,128)(2,1)} %get-tuple-element.4) | data formatting | bytes 73728
  28.4 1.2 %copy.16 = bf16[1,256]{1,0:T(2,128)(2,1)} copy(bf16[1,256]{1,0:T(2,128)(2,1)} %get-tuple-element.5) | data formatting | bytes 1024

commit v2 on v1

--- a/solution.py
+++ b/solution.py
@@ -206,7 +206,6 @@
         mask_ref[g * requests : (g + 1) * requests, :] = live
 
     pl.semaphore_wait(barrier, n_sec + n_seq - 2)
-    loads[0].wait()
     q_copies = []
     for i, peer in enumerate(sec_peers):
         copy = pltpu.make_async_remote_copy(
@@ -221,6 +220,7 @@
         q_copies.append(copy)
 
     factor = score_scale / soft_cap
+    loads[0].wait()
     loads[1].wait()
     loads[2].wait()
     pair_count = sq_ref.shape[0]
@@ -270,14 +270,17 @@
     blocks = share // HD
     lane = lax.broadcasted_iota(jnp.int32, (requests, HD), 1)
     a_copies = []
-    half = n_seq // 2
-    order = [half]
-    for i in range(1, half):
-        order += [half + i, half - i]
-    order.append(0)
+    far = deep // ((n_deep + 1) // 2)
+    mirrored = (1 - far) * (n_deep - 1 - deep) + far * deep
+    order = []
+    for t in range(n_deep - 1):
+        at = t + (t - mirrored + n_deep) // n_deep
+        at = (1 - far) * (n_deep - 1 - at) + far * at
+        order += [2 * at, 2 * at + 1]
+    order += [mate, seq]
     mask = mask_ref[...]
-    for step, offset in enumerate(order):
-        dest = lax.rem(seq + offset, n_seq) if offset else seq
+    for step, dest in enumerate(order):
+        offset = n_seq - 1 - step
         total_block = jnp.zeros((requests, HD), jnp.float32)
         for a in range(heads):
             at = pl.multiple_of(dest * share + a * G * HD, G * HD)
@@ -315,9 +318,9 @@
             ).astype(jnp.bfloat16)
             copy = pltpu.make_async_remote_copy(
                 src_ref=part_send.at[step],
-                dst_ref=part_recv.at[n_seq - offset],
+                dst_ref=part_recv.at[seq],
                 send_sem=a_send_sem.at[step],
-                recv_sem=a_recv_sem.at[n_seq - offset],
+                recv_sem=a_recv_sem.at[seq],
                 device_id={"seq": dest},
                 device_id_type=MESH,
             )
@@ -327,22 +330,20 @@
             part_own[:, share : share + HD] = jnp.where(lane < blocks, total_block, 0.0)
 
     gathered = part_own[...]
-    for copy, offset in zip(a_copies, order):
+    for peer in order[:-1]:
         pltpu.make_async_remote_copy(
             src_ref=part_send.at[0],
-            dst_ref=part_recv.at[offset],
+            dst_ref=part_recv.at[peer],
             send_sem=a_send_sem.at[0],
-            recv_sem=a_recv_sem.at[offset],
+            recv_sem=a_recv_sem.at[peer],
             device_id={"seq": seq_peers[0]},
             device_id_type=MESH,
         ).wait_recv()
-        gathered = gathered + part_recv[offset].astype(jnp.float32)
+        gathered = gathered + part_recv[peer].astype(jnp.float32)
 
     totals_part = gathered[:, share : share + HD]
     totals_part = totals_part + pltpu.roll(totals_part, HD - blocks, 1)
-    repeated = totals_part
-    for i in range(1, 2):
-        repeated = jnp.where(lane < blocks, repeated, pltpu.roll(totals_part, blocks, 1))
+    repeated = jnp.where(lane < blocks, totals_part, pltpu.roll(totals_part, blocks, 1))
     high = repeated.astype(jnp.bfloat16).astype(jnp.float32)
     tail_block = jnp.where(lane < blocks, high, repeated - high)
     sec_buf[0, :, 0:share] = gathered[:, 0:share].astype(jnp.bfloat16)
@@ -471,8 +472,8 @@
     return pl.pallas_call(
         functools.partial(decode_kernel, n_sec, n_seq, page_len),
         out_shape=(
-            jax.ShapeDtypeStruct(long_resid.shape, bf16),
-            jax.ShapeDtypeStruct(short_queries.shape, bf16),
+            pltpu.VMEM(long_resid.shape, bf16),
+            pltpu.VMEM(short_queries.shape, bf16),
         ),
         in_specs=[vmem, hbm, hbm, vmem, smem, vmem, hbm, hbm, smem, hbm, vmem],
         out_specs=(vmem, vmem),

time: 29.9 us -> 26.7 us (0.89)
  Pallas kernels: 26.4 us -> 24.7 us
  local copies, waits for them, and re-layouts: 2.58 us -> 1.18 us
    pallas_call x1, Pallas kernels: 26.4 us -> 24.7 us  [per_device_fused(): pl.pallas_call(functools.partial(decode_kernel, n_sec, n_seq, page_len),...]
    unnamed x2, local copies, waits for them, and re-layouts: 2.58 us -> 1.18 us
where the time goes in v2:
time: 26.7 us; the launch traced here: 26.5 us
  Pallas kernels  24.7 us (93%)
  local copies, waits for them, and re-layouts  1.18 us (4%)
  between operations  0.64 us (2%)
    pallas_call x1, Pallas kernels, per_device_fused(): pl.pallas_call(functools.partial(decode_kernel, n_sec, n_seq, page_len),...  24.7 us
    unnamed x2, local copies, waits for them, and re-layouts  1.18 us

profile of v2, /device:TPU:0, one launch (start us, length us, event | category | flops | bytes accessed | tf_op | source)
XLA Modules:
  0.0 26.5 jit_solution(4282909442934884348)
XLA Ops:
  0.6 24.7 %shard_map.122 = (bf16[16,1152]{1,0:T(8,128)(2,1)S(1)}, bf16[1,256]{1,0:T(2,128)(2,1)S(1)}) custom-call(bf16[4,4096]{1,0:T(4,128)(2,1)} %q_ref.1, bf16[256,2048]{1,0:T(8,128)(2,1)} %bitcast.4, bf16[256,2048]{1,0:T(8,128)(2,1)} %bitcast.5, s32[16,32]{1,0:T(8,128)} %table_ref.1, s32[16]{0:T(128)} %lens_ref.1, bf16[1,256]{1,0:T(2,128)(2,1)} %sq_ref.1, ...), custom_call_target="tpu_custom_call" | custom-call | tf_op jit(solution)/shard_map/pallas_call | solution.py:472
  25.3 0.6 %copy.15 = bf16[16,1152]{1,0:T(8,128)(2,1)} copy(bf16[16,1152]{1,0:T(8,128)(2,1)S(1)} %get-tuple-element.2) | data formatting | bytes 73728
  25.9 0.6 %copy.16 = bf16[1,256]{1,0:T(2,128)(2,1)} copy(bf16[1,256]{1,0:T(2,128)(2,1)S(1)} %get-tuple-element.3) | data formatting | bytes 1024

commit v3 on v2

--- a/solution.py
+++ b/solution.py
@@ -112,19 +112,24 @@
     n_sec,
     n_seq,
     page_len,
-    q_ref,
+    q_hbm,
     k_hbm,
     v_hbm,
+    table_hbm,
+    lens_hbm,
+    sq_hbm,
+    sk_hbm,
+    sv_hbm,
+    slens_hbm,
+    w_hbm,
+    resid_hbm,
+    long_ref,
+    short_ref,
     table_ref,
     lens_ref,
     sq_ref,
-    sk_hbm,
-    sv_hbm,
     slens_ref,
-    w_hbm,
     resid_ref,
-    long_ref,
-    short_ref,
     k_ref,
     v_ref,
     sk_ref,
@@ -173,19 +178,24 @@
     loads = []
     for i, (src, dst) in enumerate(
         (
-            (q_ref, q_slabs.at[sec]),
+            (q_hbm, q_slabs.at[sec]),
+            (table_hbm, table_ref),
+            (lens_hbm, lens_ref),
+            (sq_hbm, sq_ref),
+            (slens_hbm, slens_ref),
             (sk_hbm, sk_ref),
             (sv_hbm, sv_ref),
             (k_hbm, k_ref),
             (v_hbm, v_ref),
             (w_hbm, w_ref),
+            (resid_hbm, resid_ref),
         )
     ):
         copy = pltpu.make_async_copy(src, dst, load_sem.at[i])
         copy.start()
         loads.append(copy)
 
-    slab_rows = q_ref.shape[0]
+    slab_rows = q_hbm.shape[0]
     requests, slots = table_ref.shape
     tokens = k_ref.shape[0]
     page_count = tokens // page_len
@@ -194,6 +204,8 @@
     row = lax.broadcasted_iota(jnp.int32, (requests, tokens), 0)
     page_of = first_page + token // page_len
     slot_of = jnp.full((requests, tokens), 1 << 20, jnp.int32)
+    loads[1].wait()
+    loads[2].wait()
     table = table_ref[...]
     for s in range(slots):
         slot_of = jnp.where(table[:, s : s + 1] == page_of, s, slot_of)
@@ -205,11 +217,12 @@
     for g in range(G):
         mask_ref[g * requests : (g + 1) * requests, :] = live
 
+    loads[0].wait()
     pl.semaphore_wait(barrier, n_sec + n_seq - 2)
     q_copies = []
     for i, peer in enumerate(sec_peers):
         copy = pltpu.make_async_remote_copy(
-            src_ref=q_ref,
+            src_ref=q_slabs.at[sec],
             dst_ref=q_slabs.at[sec],
             send_sem=q_send_sem.at[i],
             recv_sem=q_recv_sem.at[sec],
@@ -220,9 +233,8 @@
         q_copies.append(copy)
 
     factor = score_scale / soft_cap
-    loads[0].wait()
-    loads[1].wait()
-    loads[2].wait()
+    for i in range(3, 7):
+        loads[i].wait()
     pair_count = sq_ref.shape[0]
     length = sk_ref.shape[0] // pair_count
     short_at = lax.broadcasted_iota(jnp.int32, (8, length), 1)
@@ -251,11 +263,11 @@
         for g in range(G):
             short_ref[p : p + 1, g * HD : (g + 1) * HD] = result[g : g + 1, :]
 
-    loads[3].wait()
-    loads[4].wait()
+    loads[7].wait()
+    loads[8].wait()
     for i, peer in enumerate(sec_peers):
         pltpu.make_async_remote_copy(
-            src_ref=q_ref,
+            src_ref=q_slabs.at[sec],
             dst_ref=q_slabs.at[peer],
             send_sem=q_send_sem.at[i],
             recv_sem=q_recv_sem.at[peer],
@@ -362,7 +374,8 @@
         b_copies.append(copy)
     sums_now = gathered[:, 0:share]
     totals_now = jnp.where(lane < blocks, totals_part, 0.0)
-    loads[5].wait()
+    loads[9].wait()
+    loads[10].wait()
     for i in range(1, n_sec):
         pltpu.make_async_remote_copy(
             src_ref=sec_buf.at[0],
@@ -466,7 +479,6 @@
     packed = share + HD
     bf16, f32 = jnp.bfloat16, jnp.float32
     vmem = pl.BlockSpec(memory_space=pltpu.VMEM)
-    smem = pl.BlockSpec(memory_space=pltpu.SMEM)
     hbm = pl.BlockSpec(memory_space=pltpu.HBM)
     dma = pltpu.SemaphoreType.DMA
     return pl.pallas_call(
@@ -475,9 +487,14 @@
             pltpu.VMEM(long_resid.shape, bf16),
             pltpu.VMEM(short_queries.shape, bf16),
         ),
-        in_specs=[vmem, hbm, hbm, vmem, smem, vmem, hbm, hbm, smem, hbm, vmem],
+        in_specs=[hbm] * 11,
         out_specs=(vmem, vmem),
         scratch_shapes=[
+            pltpu.VMEM(page_table.shape, jnp.int32),
+            pltpu.SMEM(long_lengths.shape, jnp.int32),
+            pltpu.VMEM(short_queries.shape, bf16),
+            pltpu.SMEM(short_lengths.shape, jnp.int32),
+            pltpu.VMEM(long_resid.shape, bf16),
             pltpu.VMEM((tokens, kv_width), bf16),
             pltpu.VMEM((tokens, kv_width), bf16),
             pltpu.VMEM((pair_count * length, HD), bf16),
@@ -494,7 +511,7 @@
             pltpu.VMEM((rows, columns), bf16),
             pltpu.VMEM((n_seq // 2, rows, columns), bf16),
             pltpu.VMEM((2, rows, columns), bf16),
-            dma((6,)),
+            dma((11,)),
             dma((n_sec,)),
             dma((n_sec,)),
             dma((n_seq,)),

time: 26.7 us -> 25.8 us (0.966)
  Pallas kernels: 24.7 us -> 23.9 us
    pallas_call x1, Pallas kernels: 24.7 us -> 23.9 us  [per_device_fused(): pl.pallas_call(functools.partial(decode_kernel, n_sec, n_seq, page_len),...]
where the time goes in v3:
time: 25.8 us; the launch traced here: 25.7 us
  Pallas kernels  23.9 us (93%)
  local copies, waits for them, and re-layouts  1.18 us (5%)
  between operations  0.64 us (2%)
    pallas_call x1, Pallas kernels, per_device_fused(): pl.pallas_call(functools.partial(decode_kernel, n_sec, n_seq, page_len),...  23.9 us
    unnamed x2, local copies, waits for them, and re-layouts  1.18 us

profile of v3, /device:TPU:0, one launch (start us, length us, event | category | flops | bytes accessed | tf_op | source)
XLA Modules:
  0.0 25.7 jit_solution(7570313542512729155)
XLA Ops:
  0.6 23.9 %shard_map.122 = (bf16[16,1152]{1,0:T(8,128)(2,1)S(1)}, bf16[1,256]{1,0:T(2,128)(2,1)S(1)}) custom-call(bf16[4,4096]{1,0:T(4,128)(2,1)} %q_hbm.1, bf16[256,2048]{1,0:T(8,128)(2,1)} %bitcast.4, bf16[256,2048]{1,0:T(8,128)(2,1)} %bitcast.5, s32[16,32]{1,0:T(8,128)} %table_hbm.1, s32[16]{0:T(128)} %lens_hbm.1, bf16[1,256]{1,0:T(2,128)(2,1)} %sq_hbm.1, ...), custom_call_target="tpu_custom_call" | custom-call | tf_op jit(solution)/shard_map/pallas_call | solution.py:484
  24.5 0.6 %copy.15 = bf16[16,1152]{1,0:T(8,128)(2,1)} copy(bf16[16,1152]{1,0:T(8,128)(2,1)S(1)} %get-tuple-element.2) | data formatting | bytes 73728
  25.1 0.6 %copy.16 = bf16[1,256]{1,0:T(2,128)(2,1)} copy(bf16[1,256]{1,0:T(2,128)(2,1)S(1)} %get-tuple-element.3) | data formatting | bytes 1024
